TPU v7x, 256 devices: a whole 4x4x8 slice. The times are simulated.
256 devices in a mesh: head: 4 (over x), blk: 64 (over y, z, core).
Axes of the slice: x: 4, y: 4, z: 8, core: 2. Of those that a mesh axis runs over, the one named last changes fastest.
Arguments:
- doc_x: bfloat16 [65536, 1024], P('blk'), may hold values from -6 to 6
- doc_seg: int32 [65536], P('blk'), may hold values from 0 to 1023, as said below
- doc_query: int32 [1024], replicated, may hold values from 0 to 7
- doc_var: int32 [65536], P('blk'), may hold values from 0 to 7
- query_len: int32 [8], replicated, may hold values from 256 to 4096, as said below
- block_perm: int32 [64], replicated, may hold values from 0 to 63, each once
- cache_k: bfloat16 [32768, 1024], P('blk', 'head'), may hold values from -164 to 164
- cache_v: bfloat16 [32768, 1024], P('blk', 'head'), may hold values from -6 to 6
- cache_var: int32 [32768], P('blk'), may hold values from 0 to 7
- w_query: bfloat16 [1024, 1024], P(None, 'head'), may hold values from -0.1875 to 0.1875
- w_key: bfloat16 [1024, 1024], P(None, 'head'), may hold values from -0.5 to 0.5
- w_value: bfloat16 [1024, 1024], P(None, 'head'), may hold values from -0.1875 to 0.1875
- w_out: bfloat16 [1024, 1024], P('head'), may hold values from -0.1875 to 0.1875
- var_bias: float32 [2, 16], P(None, 'head'), may hold values from -1 to 1
- norm_gain: float32 [1024], replicated, may hold values from 0.1 to 1.9
- readout: float32 [1024], replicated, may hold values from -1.5 to 1.5
Outputs:
- update: float32 [65536, 1024], P('blk', 'head')
- pooled: float32 [1024], P('blk')
Inputs may be any that keep to these rules, and one draw needn't show every extreme that they name: `doc_seg`: index i of blk holds documents i * 16 to (i + 1) * 16 - 1 whole; its 1024 tokens form 8 runs of 128 tokens, run j holding its documents 2j and 2j + 1, both of one query, and the 8 runs of one index belong to 8 different queries. query_len[0] = 4096.
All inputs are finite; a program needn't handle non-finite values.
Results may differ from a plain program's by a relative error of at most 0.012.
The roundings to bfloat16 on the way count: a program that leaves them out, or rounds other values in their place, can miss the bound.
Values may be sent and summed in bfloat16 or wider, within the bound.
A program may use at most 128 MiB of HBM per device.

v0:
```python
import jax
import jax.numpy as jnp
from jax import lax
from jax.sharding import PartitionSpec as P

D = 1024
DH = 64
QUERIES = 8


def rotary(projected, positions):
    row_count = projected.shape[0]
    head_count = projected.shape[1] // DH
    half_size = DH // 2
    shaped = projected.reshape(row_count, head_count, DH)
    frequency = 10000.0 ** (-jnp.arange(half_size, dtype=jnp.float32) / half_size)
    angles = positions.astype(jnp.float32)[:, None] * frequency[None, :]
    cosine = jnp.cos(angles)[:, None, :]
    sine_part = jnp.sin(angles)[:, None, :]
    first_half = shaped[:, :, :half_size]
    second_half = shaped[:, :, half_size:]
    turned = jnp.concatenate(
        [
            first_half * cosine - second_half * sine_part,
            second_half * cosine + first_half * sine_part,
        ],
        axis=2,
    )
    return turned.reshape(row_count, head_count * DH)


def softmax_part(scores, allowed):
    scores = jnp.where(allowed, scores, -1e30)
    peak = jnp.max(scores, axis=-1)
    weights = jnp.where(allowed, jnp.exp(scores - peak[..., None]), 0.0)
    return (peak, jnp.sum(weights, axis=-1), weights.astype(jnp.bfloat16))


def cache_part(
    recv_q, recv_var, cache_keys, cache_values, cache_var, row_valid, bias_same, bias_other
):
    source_count = recv_q.shape[0]
    item_count = recv_q.shape[1]
    col_count = recv_q.shape[2]
    head_count = cache_keys.shape[1]
    total_rows = source_count * item_count
    block_rows = 512
    block_count = total_rows // block_rows
    flat_q = recv_q.reshape(block_count, block_rows, head_count, DH)
    flat_var = recv_var.reshape(block_count, block_rows).astype(jnp.int32)

    def one_block(block_inputs):
        block_q, block_var = block_inputs
        scores = (
            jnp.einsum("thd,rhd->htr", block_q, cache_keys, preferred_element_type=jnp.float32)
            * 0.125
        )
        scores = scores + jnp.where(
            (block_var[:, None] == cache_var[None, :])[None], bias_same, bias_other
        )
        allowed = jnp.broadcast_to(row_valid[None, None, :], scores.shape)
        peak, total_weight, weights = softmax_part(scores, allowed)
        mixed = jnp.einsum(
            "htr,rhd->thd", weights, cache_values, preferred_element_type=jnp.float32
        )
        return (peak.T, total_weight.T, mixed.reshape(block_rows, col_count))

    maxima, totals, sums = lax.map(one_block, (flat_q, flat_var))
    return (
        maxima.reshape(source_count, item_count, head_count),
        totals.reshape(source_count, item_count, head_count),
        sums.reshape(source_count, item_count, col_count),
    )


def body(
    doc_x,
    doc_seg,
    doc_query,
    doc_var,
    query_len,
    block_perm,
    cache_k,
    cache_v,
    cache_var,
    w_query,
    w_key,
    w_value,
    w_out,
    var_bias,
    norm_gain,
    readout,
):
    row_count = doc_x.shape[0]
    col_count = w_query.shape[1]
    head_count = col_count // DH
    cache_count = cache_k.shape[0]
    blk_count = lax.axis_size("blk")
    blk_index = lax.axis_index("blk")
    head_index = lax.axis_index("head")
    blocks_each = blk_count // QUERIES
    slot_count = QUERIES
    slot_rows = row_count // slot_count
    doc_count = 2 * slot_count
    first_doc = blk_index * doc_count
    local_seg = doc_seg - first_doc
    member = (local_seg[:, None] == jnp.arange(doc_count, dtype=jnp.int32)[None, :]).astype(
        jnp.int32
    )
    lengths = jnp.sum(member, axis=0)
    starts = jnp.cumsum(lengths) - lengths
    first_pos = jnp.dot(member, starts)
    own_docs_query = lax.dynamic_slice_in_dim(doc_query, first_doc, doc_count)
    query_table = (own_docs_query[:, None] == jnp.arange(QUERIES, dtype=jnp.int32)[None, :]).astype(
        jnp.int32
    )
    doc_len = jnp.sum(query_table * query_len[None, :], axis=1)
    tok_len = jnp.dot(member, doc_len)
    positions = tok_len + jnp.arange(row_count, dtype=jnp.int32) - first_pos
    query_rot = rotary(
        jnp.dot(doc_x, w_query, preferred_element_type=jnp.float32), positions
    ).astype(jnp.bfloat16)
    key_rot = rotary(jnp.dot(doc_x, w_key, preferred_element_type=jnp.float32), positions).astype(
        jnp.bfloat16
    )
    value_proj = jnp.dot(doc_x, w_value, preferred_element_type=jnp.float32).astype(jnp.bfloat16)
    bias_same = var_bias[0][:, None, None]
    bias_other = var_bias[1][:, None, None]
    shaped_q = query_rot.reshape(slot_count, slot_rows, head_count, DH)
    shaped_k = key_rot.reshape(slot_count, slot_rows, head_count, DH)
    shaped_v = value_proj.reshape(slot_count, slot_rows, head_count, DH)
    slot_seg = local_seg.reshape(slot_count, slot_rows)
    slot_var = doc_var.reshape(slot_count, slot_rows)
    self_scores = (
        jnp.einsum("gthd,gshd->ghts", shaped_q, shaped_k, preferred_element_type=jnp.float32)
        * 0.125
    )
    self_scores = self_scores + jnp.where(
        (slot_var[:, :, None] == slot_var[:, None, :])[:, None], bias_same[None], bias_other[None]
    )
    self_allowed = (slot_seg[:, :, None] == slot_seg[:, None, :])[:, None]
    self_peak, self_total, self_weights = softmax_part(self_scores, self_allowed)
    self_sum = jnp.einsum(
        "ghts,gshd->gthd", self_weights, shaped_v, preferred_element_type=jnp.float32
    )
    self_peak = self_peak.transpose(0, 2, 1)
    self_total = self_total.transpose(0, 2, 1)
    slot_query = own_docs_query.reshape(slot_count, 2)[:, 0]
    block_query = block_perm // blocks_each
    slot_match = block_query[:, None] == slot_query[None, :]
    slot_pick = jnp.sum(
        slot_match.astype(jnp.int32) * jnp.arange(slot_count, dtype=jnp.int32)[None, :], axis=1
    )
    send_q = jnp.take(query_rot.reshape(slot_count, slot_rows, col_count), slot_pick, axis=0)
    send_var = jnp.take(slot_var, slot_pick, axis=0).astype(jnp.bfloat16)
    my_block = lax.dynamic_slice_in_dim(block_perm, blk_index, 1)[0]
    my_query = my_block // blocks_each
    first_row = my_block % blocks_each * cache_count
    my_len = lax.dynamic_slice_in_dim(query_len, my_query, 1)[0]
    row_valid = first_row + jnp.arange(cache_count, dtype=jnp.int32) < my_len
    cache_keys = cache_k.reshape(cache_count, head_count, DH)
    cache_values = cache_v.reshape(cache_count, head_count, DH)
    recv_q, recv_var = (
        lax.all_to_all(send_q, "blk", split_axis=0, concat_axis=0, tiled=True),
        lax.all_to_all(send_var, "blk", split_axis=0, concat_axis=0, tiled=True),
    )
    maxima, totals, sums = cache_part(
        recv_q, recv_var, cache_keys, cache_values, cache_var, row_valid, bias_same, bias_other
    )
    got_max, got_total, got_sum = (
        lax.all_to_all(maxima, "blk", split_axis=0, concat_axis=0, tiled=True),
        lax.all_to_all(totals, "blk", split_axis=0, concat_axis=0, tiled=True),
        lax.all_to_all(sums, "blk", split_axis=0, concat_axis=0, tiled=True),
    )
    match_float = slot_match.astype(jnp.float32)
    spread_max = jnp.where(slot_match[:, :, None, None], got_max[:, None], -1e30)
    cache_peak = jnp.max(spread_max, axis=0)
    peak = jnp.maximum(cache_peak, self_peak)
    device_peak = jnp.take(peak, slot_pick, axis=0)
    factor = jnp.exp(got_max - device_peak)
    cache_total = jnp.einsum(
        "dg,dth->gth", match_float, got_total * factor, precision=lax.Precision.HIGHEST
    )
    scaled_sum = got_sum.reshape(blk_count, slot_rows, head_count, DH) * factor[..., None]
    cache_sum = jnp.einsum(
        "dg,dthe->gthe", match_float, scaled_sum, precision=lax.Precision.HIGHEST
    )
    self_factor = jnp.exp(self_peak - peak)
    numerator = cache_sum + self_sum * self_factor[..., None]
    denominator = cache_total + self_total * self_factor
    attended = (
        (numerator / denominator[..., None]).reshape(row_count, col_count).astype(jnp.bfloat16)
    )
    partial_update = jnp.dot(attended, w_out, preferred_element_type=jnp.float32)
    x_float = doc_x.astype(jnp.float32)
    whole_sum = lax.psum(partial_update, "head")
    hidden = x_float + whole_sum
    square_sum = jnp.sum(hidden * hidden, axis=1)
    weighted = jnp.sum(hidden * norm_gain * readout, axis=1)
    update = lax.dynamic_slice_in_dim(whole_sum, head_index * col_count, col_count, 1)
    token_score = weighted * lax.rsqrt(square_sum / D + 1e-06)
    pooled_sum = jnp.dot(token_score, member.astype(jnp.float32), precision=lax.Precision.HIGHEST)
    return (update, pooled_sum / lengths.astype(jnp.float32))


def solution(mesh):
    return jax.shard_map(
        body,
        mesh=mesh,
        in_specs=(
            P("blk", None),
            P("blk"),
            P(),
            P("blk"),
            P(),
            P(),
            P("blk", "head"),
            P("blk", "head"),
            P("blk"),
            P(None, "head"),
            P(None, "head"),
            P(None, "head"),
            P("head", None),
            P(None, "head"),
            P(),
            P(),
        ),
        out_specs=(P("blk", "head"), P("blk")),
        check_vma=False,
    )
```

profile of v0, /device:TPU:1, one launch (start us, length us, event | category | flops | bytes accessed | tf_op | source)
XLA Modules:
  0.0 646.7 jit_solution(2000789111802115484)
XLA Ops:
  11.0 13.2 %all-to-all-start.1 = ((bf16[64,1,128]{2,1,0:T(2,128)(2,1)}), bf16[64,1,128]{2,1,0:T(2,128)(2,1)S(1)}, u32[]{:S(2)}, u32[]{:S(2)}) async-start(bf16[64,1,128]{2,1,0:T(2,128)(2,1)} %copy.100), calls=%async_computation.1 | async-start | bytes 65536 | tf_op jit(solution)/shard_map/all_to_all | solution.py:165
  26.4 2.4 fusion.63
  30.1 2.8 gather_fusion
  32.8 4.6 broadcast_select_fusion
  37.4 10.7 %all-to-all-start = ((bf16[64,128,256]{2,1,0:T(8,128)(2,1)}), bf16[64,128,256]{2,1,0:T(8,128)(2,1)}, u32[]{:S(2)}, u32[]{:S(2)}) async-start(bf16[64,128,256]{2,1,0:T(8,128)(2,1)} %broadcast_select_fusion), calls=%async_computation | async-start | bytes 8388608 | tf_op jit(solution)/shard_map/all_to_all | solution.py:164
  53.1 90.9 %all-to-all-done = bf16[64,128,256]{2,1,0:T(8,128)(2,1)} async-done(((bf16[64,128,256]{2,1,0:T(8,128)(2,1)}), bf16[64,128,256]{2,1,0:T(8,128)(2,1)}, u32[]{:S(2)}, u32[]{:S(2)}) %all-to-all-start) | async-done | bytes 4194336 | tf_op jit(solution)/shard_map/all_to_all | solution.py:164
  144.0 12.9 %reshape.307 = bf16[16,512,4,64]{3,2,1,0:T(4,128)(2,1)} reshape(bf16[64,128,256]{2,1,0:T(8,128)(2,1)} %all-to-all-done) | data formatting | bytes 8388608 | tf_op jit(solution)/shard_map/reshape | solution.py:49
  156.9 12.7 %copy.102 = bf16[16,512,4,64]{1,3,2,0:T(8,128)(2,1)} copy(bf16[16,512,4,64]{3,2,1,0:T(4,128)(2,1)} %reshape.307) | data formatting | bytes 8388608
  169.6 122.0 %while.15 = (s32[]{:T(128)}, f32[16,512,4]{1,2,0:T(4,128)S(1)}, f32[16,512,4]{1,2,0:T(4,128)S(1)}, f32[16,512,256]{2,1,0:T(8,128)}, bf16[16,512,4,64]{1,3,2,0:T(...) while((s32[]{:T(128)}, f32[16,512,4]{1,2,0:T(4,128)S(1)}, ...), condition=%wide.region_7.8_spmd.clone, body=%wide.region_4.7_spmd.clone.sunk | while | flops 288617472 | bytes 17115396 | solution.py:68
  170.6 2.5 fusion.87
  173.0 1.5 fusion.88
  174.5 1.7 fusion.89
  178.2 2.4 fusion.87
  180.7 1.5 fusion.88
  182.1 1.7 fusion.89
  185.9 2.4 fusion.87
  188.3 1.5 fusion.88
  189.8 1.7 fusion.89
  193.5 2.5 fusion.87
  195.9 1.5 fusion.88
  197.4 1.7 fusion.89
  201.1 2.5 fusion.87
  203.5 1.5 fusion.88
  205.0 1.7 fusion.89
  208.7 2.5 fusion.87
  211.1 1.5 fusion.88
  212.6 1.7 fusion.89
  216.3 2.5 fusion.87
  220.3 1.7 fusion.89
  223.9 2.5 fusion.87
  227.9 1.7 fusion.89
  231.5 2.5 fusion.87
  235.5 1.7 fusion.89
  239.2 2.4 fusion.87
  243.1 1.7 fusion.89
  246.8 2.5 fusion.87
  249.3 1.5 fusion.88
  250.8 1.7 fusion.89
  254.4 2.5 fusion.87
  258.4 1.7 fusion.89
  262.0 2.5 fusion.87
  266.0 1.7 fusion.89
  269.6 2.5 fusion.87
  272.1 1.5 fusion.88
  273.6 1.7 fusion.89
  277.3 2.5 fusion.87
  281.2 1.7 fusion.89
  284.9 2.5 fusion.87
  288.8 1.7 fusion.89
  291.6 16.0 %all_to_all.26 = f32[64,128,4]{1,2,0:T(4,128)} all-to-all(f32[64,128,4]{1,2,0:T(4,128)S(1)} %bitcast.155), channel_id=1, replica_groups=mesh['head'=4,'blk'=64] {'blk'}, dimensions={0} | all-to-all | bytes 262144 | tf_op jit(solution)/shard_map/all_to_all | solution.py:172
  307.6 15.0 %all_to_all.27 = f32[64,128,4]{1,2,0:T(4,128)S(1)} all-to-all(f32[64,128,4]{1,2,0:T(4,128)S(1)} %bitcast.154), channel_id=1, replica_groups=mesh['head'=4,'blk'=64] {'blk'}, dimensions={0} | all-to-all | bytes 262144 | tf_op jit(solution)/shard_map/all_to_all | solution.py:171
  322.6 5.6 all-to-all-start.2
  330.0 2.5 convolution_convert_fusion
  332.5 2.8 reshape.308
  335.7 1.8 fusion.64
  339.0 1.5 fusion.28
  342.1 172.0 %all-to-all-done.2 = f32[64,128,256]{2,1,0:T(8,128)} async-done(((f32[64,128,256]{2,1,0:T(8,128)}), f32[64,128,256]{2,1,0:T(8,128)}, u32[]{:S(2)}, u32[]{:S(2)}) %all-to-all-start.2) | async-done | bytes 8388640 | tf_op jit(solution)/shard_map/all_to_all | solution.py:173
  514.1 9.0 %copy.104 = f32[64,128,256]{1,2,0:T(8,128)} copy(f32[64,128,256]{2,1,0:T(8,128)} %all-to-all-done.2) | data formatting | bytes 16777216 | tf_op jit(solution)/shard_map/all_to_all | solution.py:173
  523.0 4.6 broadcast_multiply_fusion
  527.7 8.5 %fusion.24 = bf16[8,128,4,64]{1,0,3,2:T(8,128)(2,1)S(1)} fusion(f32[64,128,4,64]{1,3,2,0:T(8,128)S(1)} %broadcast_multiply_fusion, f32[8,4,64,128]{3,2,1,0:T(8,128)S(1)} %copy-done.3, f32[8,128,4]{1,0,2:T(8,128)S(1)} %convolution_add_fusion, f32[8,128,4]{1,0,2:T(8,128)S(1)} %get-tuple-element.189, s32[64]{0:T(128)S(1)} %copy-done.16, s32[8]{0:T(128)S(1)} %copy-done.13), kind=kOutput, calls=%fused_computation.36 | convolution fusion | flops 202375680 | bytes 9994528 | tf_op jit(solution)/shard_map/dg,dthe->gthe/dot_general | solution.py:185
  536.2 2.7 fusion.34
  539.0 94.6 %all-reduce.2.cloned.1.call-done = f32[1024,1024]{1,0:T(8,128)} async-done(((f32[1024,1024]{1,0:T(8,128)}), f32[1024,1024]{1,0:T(8,128)}) %all-reduce.2.cloned.1.call-update) | async-done | bytes 4194320 | tf_op jit(solution)/shard_map/psum | solution.py:196
  633.6 3.3 multiply_reduce_fusion
  637.6 2.3 constant_dynamic-slice_fusion.1
  (215 shorter events, 58.6 us)
Async XLA Ops:
  7.2 529.0 %copy-start = (bf16[256,1024]{1,0:T(8,128)(2,1)S(1)}, bf16[256,1024]{1,0:T(8,128)(2,1)}, u32[]{:S(2)}) copy-start(bf16[256,1024]{1,0:T(8,128)(2,1)} %param.30) | copy-start | bytes 1572868
  7.9 320.7 %copy-start.15 = (s32[64]{0:T(128)}, s32[64]{0:T(128)S(1)}, u32[]{:S(2)}) copy-start(s32[64]{0:T(128)S(1)} %and_select_fusion) | copy-start | bytes 772
  8.9 319.7 %copy-start.12 = (s32[8]{0:T(128)}, s32[8]{0:T(128)S(1)}, u32[]{:S(2)}) copy-start(s32[8]{0:T(128)S(1)} %slice_reduce_fusion) | copy-start | bytes 100
  9.0 23.9 %copy-start.17 = (pred[64]{0:T(512)(128)(4,1)}, pred[64]{0:T(512)(128)(4,1)S(1)}, u32[]{:S(2)}) copy-start(pred[64]{0:T(512)(128)(4,1)S(1)} %compare_and_fusion) | copy-start | bytes 196
  9.0 21.1 %copy-start.14 = (s32[1024]{0:T(1024)}, s32[1024]{0:T(1024)S(1)}, u32[]{:S(2)}) copy-start(s32[1024]{0:T(1024)S(1)} %pad_clamp_fusion) | copy-start | bytes 12292
  11.0 26.4 %all-to-all-start.1 = ((bf16[64,1,128]{2,1,0:T(2,128)(2,1)}), bf16[64,1,128]{2,1,0:T(2,128)(2,1)S(1)}, u32[]{:S(2)}, u32[]{:S(2)}) async-start(bf16[64,1,128]{2,1,0:T(2,128)(2,1)} %copy.100), calls=%async_computation.1 | async-start | bytes 65536 | tf_op jit(solution)/shard_map/all_to_all | solution.py:165
  24.9 4.8 copy-start.10
  25.0 0.5 copy-start.21
  37.4 10.7 %copy-start.26 = (s32[64]{0:T(128)S(1)}, s32[64]{0:T(128)}, u32[]{:S(2)}) copy-start(s32[64]{0:T(128)} %param.23) | copy-start | bytes 772
  37.4 13.9 %copy-start.6 = (bf16[512,256]{1,0:T(8,128)(2,1)S(1)}, bf16[512,256]{1,0:T(8,128)(2,1)}, u32[]{:S(2)}) copy-start(bf16[512,256]{1,0:T(8,128)(2,1)} %param.24) | copy-start | bytes 786436
  37.4 14.1 %copy-start.7 = (bf16[512,256]{1,0:T(8,128)(2,1)S(1)}, bf16[512,256]{1,0:T(8,128)(2,1)}, u32[]{:S(2)}) copy-start(bf16[512,256]{1,0:T(8,128)(2,1)} %param.25) | copy-start | bytes 786436
  37.4 14.3 %copy-start.27 = (s32[8]{0:T(128)S(1)}, s32[8]{0:T(128)}, u32[]{:S(2)}) copy-start(s32[8]{0:T(128)} %param.22) | copy-start | bytes 100
  37.4 14.9 %copy-start.23 = (f32[2,4]{1,0:T(2,128)S(1)}, f32[2,4]{1,0:T(2,128)}, u32[]{:S(2)}) copy-start(f32[2,4]{1,0:T(2,128)} %param.31) | copy-start | bytes 100
  37.4 106.5 %all-to-all-start = ((bf16[64,128,256]{2,1,0:T(8,128)(2,1)}), bf16[64,128,256]{2,1,0:T(8,128)(2,1)}, u32[]{:S(2)}, u32[]{:S(2)}) async-start(bf16[64,128,256]{2,1,0:T(8,128)(2,1)} %broadcast_select_fusion), calls=%async_computation | async-start | bytes 8388608 | tf_op jit(solution)/shard_map/all_to_all | solution.py:164
  156.9 12.7 %copy-start.8 = (s32[512]{0:T(512)S(1)}, s32[512]{0:T(512)}, u32[]{:S(2)}) copy-start(s32[512]{0:T(512)} %param.26) | copy-start | bytes 6148
  322.6 7.4 %copy-start.1 = (bf16[1024,1024]{1,0:T(8,128)(2,1)S(1)}, bf16[1024,1024]{1,0:T(8,128)(2,1)}, u32[]{:S(2)}) copy-start(bf16[1024,1024]{1,0:T(8,128)(2,1)} %param.18) | copy-start | bytes 6291460
  322.6 191.5 %all-to-all-start.2 = ((f32[64,128,256]{2,1,0:T(8,128)}), f32[64,128,256]{2,1,0:T(8,128)}, u32[]{:S(2)}, u32[]{:S(2)}) async-start(f32[64,128,256]{2,1,0:T(8,128)} %bitcast.145), calls=%async_computation.2 | async-start | bytes 16777216 | tf_op jit(solution)/shard_map/all_to_all | solution.py:173
  328.3 7.0 %copy-start.9 = (s32[1024]{0:T(1024)S(1)}, s32[1024]{0:T(1024)}, u32[]{:S(2)}) copy-start(s32[1024]{0:T(1024)} %param.19) | copy-start | bytes 12292
  328.3 7.0 %copy-start.2 = (s32[1024]{0:T(1024)S(1)}, s32[1024]{0:T(1024)}, u32[]{:S(2)}) copy-start(s32[1024]{0:T(1024)} %param.21) | copy-start | bytes 12292
  328.3 305.3 %all-reduce.2.cloned.1.call-start = ((), (), s32[]{:S(2)}) async-start(), calls=%async_computation.5 | async-start | bytes 8388608 | tf_op jit(solution)/shard_map/psum | solution.py:196
  335.3 2.4 copy-start.24
  335.3 2.4 copy-start.25
  337.7 1.3 copy-start.4
  340.8 1.0 copy-start.5
  340.8 1.0 copy-start.18
  340.8 1.1 copy-start.13
  340.8 1.1 copy-start.16
  523.0 4.7 copy-start.3
  538.9 94.7 %copy-start.19 = (f32[1024]{0:T(1024)S(1)}, f32[1024]{0:T(1024)}, u32[]{:S(2)}) copy-start(f32[1024]{0:T(1024)} %param.33) | copy-start | bytes 12292
  538.9 94.7 %copy-start.20 = (f32[1024]{0:T(1024)S(1)}, f32[1024]{0:T(1024)}, u32[]{:S(2)}) copy-start(f32[1024]{0:T(1024)} %param.32) | copy-start | bytes 12292
  539.0 97.9 %copy-start.11 = (s32[1024]{0:T(1024)S(1)}, s32[1024]{0:T(1024)}, u32[]{:S(2)}) copy-start(s32[1024]{0:T(1024)} %copy-done.10) | copy-start | bytes 12292
  539.0 97.9 %copy-start.22 = (s32[16]{0:T(128)S(1)}, s32[16]{0:T(128)}, u32[]{:S(2)}) copy-start(s32[16]{0:T(128)} %copy-done.21) | copy-start | bytes 196
Sparse Core Ops, SparseCore 0:
  539.1 94.4 all-reduce.1
where the time goes:
time: 649 us; the launch traced here: 647 us
  waiting for transfers between devices  358 us (55%)
  matrix products  87.6 us (13%)
  local copies, waits for them, and re-layouts  66.9 us (10%)
  other arithmetic  56 us (9%)
  blocking collectives  31 us (5%)
  starting transfers between devices  29.7 us (5%)
  between operations  17.2 us (3%)
    all_to_all x1, waiting for transfers between devices, body(): lax.all_to_all(sums, 'blk', split_axis=0, concat_axis=0, tiled=True)  172 us
    psum x1, waiting for transfers between devices, body(): whole_sum = lax.psum(partial_update, 'head')  94.6 us
    all_to_all x1, waiting for transfers between devices, body(): lax.all_to_all(send_q, 'blk', split_axis=0, concat_axis=0, tiled=True)  90.9 us
    dot_general x16, matrix products, one_block(): jnp.einsum('thd,rhd->htr', block_q, cache_keys, preferred_element_type=jn...  39.2 us
    dot_general x16, matrix products, one_block(): jnp.einsum('htr,rhd->thd', weights, cache_values, preferred_element_type=...  26.9 us
    reduce_sum x17, other arithmetic, softmax_part(): return (peak, jnp.sum(weights, axis=-1), weights.astype(jnp.bfloat16))  24 us
    dynamic_update_slice x48, local copies, waits for them, and re-layouts, cache_part(): maxima, totals, sums = lax.map(one_block, (flat_q, flat_var))  16.9 us
    all_to_all x1, blocking collectives, body(): lax.all_to_all(totals, 'blk', split_axis=0, concat_axis=0, tiled=True)  16 us
  transfers between devices with their start and end apart: 4, of which 3 were waited for; matrix products, arithmetic and copies ran while one was open for 4% of the time, Pallas kernels for 0%

commit v1 on v0

--- a/solution.py
+++ b/solution.py
@@ -193,7 +193,7 @@
     )
     partial_update = jnp.dot(attended, w_out, preferred_element_type=jnp.float32)
     x_float = doc_x.astype(jnp.float32)
-    whole_sum = lax.psum(partial_update, "head")
+    whole_sum = jnp.sum(lax.all_gather(partial_update, "head"), axis=0)
     hidden = x_float + whole_sum
     square_sum = jnp.sum(hidden * hidden, axis=1)
     weighted = jnp.sum(hidden * norm_gain * readout, axis=1)

time: 649 us -> 718 us (1.11)
  waiting for transfers between devices: 358 us -> 416 us
  other arithmetic: 56 us -> 66.5 us
    all_gather x0 -> x1, waiting for transfers between devices: none -> 153 us  [body(): whole_sum = jnp.sum(lax.all_gather(partial_update, 'head'), axis=0)]
    psum x1 -> x0, waiting for transfers between devices: 94.6 us -> none  [body(): whole_sum = lax.psum(partial_update, 'head')]
    reduce_sum x0 -> x1, other arithmetic: none -> 10.5 us  [body(): whole_sum = jnp.sum(lax.all_gather(partial_update, 'head'), axis=0)]
where the time goes in v1:
time: 718 us; the launch traced here: 716 us
  waiting for transfers between devices  416 us (58%)
  matrix products  87.6 us (12%)
  local copies, waits for them, and re-layouts  66.9 us (9%)
  other arithmetic  66.5 us (9%)
  blocking collectives  31 us (4%)
  starting transfers between devices  29.7 us (4%)
  between operations  17.2 us (2%)
    all_to_all x1, waiting for transfers between devices, body(): lax.all_to_all(sums, 'blk', split_axis=0, concat_axis=0, tiled=True)  172 us
    all_gather x1, waiting for transfers between devices, body(): whole_sum = jnp.sum(lax.all_gather(partial_update, 'head'), axis=0)  153 us
    all_to_all x1, waiting for transfers between devices, body(): lax.all_to_all(send_q, 'blk', split_axis=0, concat_axis=0, tiled=True)  90.9 us
    dot_general x16, matrix products, one_block(): jnp.einsum('thd,rhd->htr', block_q, cache_keys, preferred_element_type=jn...  39.2 us
    dot_general x16, matrix products, one_block(): jnp.einsum('htr,rhd->thd', weights, cache_values, preferred_element_type=...  26.9 us
    reduce_sum x17, other arithmetic, softmax_part(): return (peak, jnp.sum(weights, axis=-1), weights.astype(jnp.bfloat16))  24 us
    dynamic_update_slice x48, local copies, waits for them, and re-layouts, cache_part(): maxima, totals, sums = lax.map(one_block, (flat_q, flat_var))  16.9 us
    all_to_all x1, blocking collectives, body(): lax.all_to_all(totals, 'blk', split_axis=0, concat_axis=0, tiled=True)  16 us
  transfers between devices with their start and end apart: 4, of which 3 were waited for; matrix products, arithmetic and copies ran while one was open for 4% of the time, Pallas kernels for 0%

profile of v1, /device:TPU:1, one launch (start us, length us, event | category | flops | bytes accessed | tf_op | source)
XLA Modules:
  0.0 716.0 jit_solution(9885027906692869637)
XLA Ops:
  11.0 13.2 %all-to-all-start.1 = ((bf16[64,1,128]{2,1,0:T(2,128)(2,1)}), bf16[64,1,128]{2,1,0:T(2,128)(2,1)S(1)}, u32[]{:S(2)}, u32[]{:S(2)}) async-start(bf16[64,1,128]{2,1,0:T(2,128)(2,1)} %copy.100), calls=%async_computation.1 | async-start | bytes 65536 | tf_op jit(solution)/shard_map/all_to_all | solution.py:165
  26.4 2.4 fusion.63
  30.1 2.8 gather_fusion
  32.8 4.6 broadcast_select_fusion
  37.4 10.7 %all-to-all-start = ((bf16[64,128,256]{2,1,0:T(8,128)(2,1)}), bf16[64,128,256]{2,1,0:T(8,128)(2,1)}, u32[]{:S(2)}, u32[]{:S(2)}) async-start(bf16[64,128,256]{2,1,0:T(8,128)(2,1)} %broadcast_select_fusion), calls=%async_computation | async-start | bytes 8388608 | tf_op jit(solution)/shard_map/all_to_all | solution.py:164
  53.1 90.9 %all-to-all-done = bf16[64,128,256]{2,1,0:T(8,128)(2,1)} async-done(((bf16[64,128,256]{2,1,0:T(8,128)(2,1)}), bf16[64,128,256]{2,1,0:T(8,128)(2,1)}, u32[]{:S(2)}, u32[]{:S(2)}) %all-to-all-start) | async-done | bytes 4194336 | tf_op jit(solution)/shard_map/all_to_all | solution.py:164
  144.0 12.9 %reshape.308 = bf16[16,512,4,64]{3,2,1,0:T(4,128)(2,1)} reshape(bf16[64,128,256]{2,1,0:T(8,128)(2,1)} %all-to-all-done) | data formatting | bytes 8388608 | tf_op jit(solution)/shard_map/reshape | solution.py:49
  156.9 12.7 %copy.102 = bf16[16,512,4,64]{1,3,2,0:T(8,128)(2,1)} copy(bf16[16,512,4,64]{3,2,1,0:T(4,128)(2,1)} %reshape.308) | data formatting | bytes 8388608
  169.6 122.0 %while.15 = (s32[]{:T(128)}, f32[16,512,4]{1,2,0:T(4,128)S(1)}, f32[16,512,4]{1,2,0:T(4,128)S(1)}, f32[16,512,256]{2,1,0:T(8,128)}, bf16[16,512,4,64]{1,3,2,0:T(...) while((s32[]{:T(128)}, f32[16,512,4]{1,2,0:T(4,128)S(1)}, ...), condition=%wide.region_7.8_spmd.clone, body=%wide.region_4.7_spmd.clone.sunk | while | flops 288617472 | bytes 17115396 | solution.py:68
  170.6 2.5 fusion.87
  173.0 1.5 fusion.88
  174.5 1.7 fusion.89
  178.2 2.4 fusion.87
  180.7 1.5 fusion.88
  182.1 1.7 fusion.89
  185.9 2.4 fusion.87
  188.3 1.5 fusion.88
  189.8 1.7 fusion.89
  193.5 2.5 fusion.87
  195.9 1.5 fusion.88
  197.4 1.7 fusion.89
  201.1 2.5 fusion.87
  205.0 1.7 fusion.89
  208.7 2.5 fusion.87
  211.1 1.5 fusion.88
  212.6 1.7 fusion.89
  216.3 2.5 fusion.87
  220.3 1.7 fusion.89
  223.9 2.5 fusion.87
  227.9 1.7 fusion.89
  231.5 2.5 fusion.87
  235.5 1.7 fusion.89
  239.2 2.4 fusion.87
  243.1 1.7 fusion.89
  246.8 2.5 fusion.87
  249.3 1.5 fusion.88
  250.8 1.7 fusion.89
  254.4 2.5 fusion.87
  258.4 1.7 fusion.89
  262.0 2.5 fusion.87
  266.0 1.7 fusion.89
  269.6 2.5 fusion.87
  272.1 1.5 fusion.88
  273.6 1.7 fusion.89
  277.3 2.5 fusion.87
  281.2 1.7 fusion.89
  284.9 2.5 fusion.87
  288.8 1.7 fusion.89
  291.6 16.0 %all_to_all.26 = f32[64,128,4]{1,2,0:T(4,128)} all-to-all(f32[64,128,4]{1,2,0:T(4,128)S(1)} %bitcast.157), channel_id=1, replica_groups=mesh['head'=4,'blk'=64] {'blk'}, dimensions={0} | all-to-all | bytes 262144 | tf_op jit(solution)/shard_map/all_to_all | solution.py:172
  307.6 15.0 %all_to_all.27 = f32[64,128,4]{1,2,0:T(4,128)S(1)} all-to-all(f32[64,128,4]{1,2,0:T(4,128)S(1)} %bitcast.156), channel_id=1, replica_groups=mesh['head'=4,'blk'=64] {'blk'}, dimensions={0} | all-to-all | bytes 262144 | tf_op jit(solution)/shard_map/all_to_all | solution.py:171
  322.6 5.6 all-to-all-start.2
  330.0 2.5 convolution_convert_fusion
  332.5 2.8 reshape.309
  335.7 1.8 fusion.64
  339.0 1.5 fusion.28
  342.1 172.0 %all-to-all-done.2 = f32[64,128,256]{2,1,0:T(8,128)} async-done(((f32[64,128,256]{2,1,0:T(8,128)}), f32[64,128,256]{2,1,0:T(8,128)}, u32[]{:S(2)}, u32[]{:S(2)}) %all-to-all-start.2) | async-done | bytes 8388640 | tf_op jit(solution)/shard_map/all_to_all | solution.py:173
  514.1 9.0 %copy.104 = f32[64,128,256]{1,2,0:T(8,128)} copy(f32[64,128,256]{2,1,0:T(8,128)} %all-to-all-done.2) | data formatting | bytes 16777216 | tf_op jit(solution)/shard_map/all_to_all | solution.py:173
  523.0 4.6 broadcast_multiply_fusion
  527.7 8.5 %fusion.24 = bf16[8,128,4,64]{1,0,3,2:T(8,128)(2,1)S(1)} fusion(f32[64,128,4,64]{1,3,2,0:T(8,128)S(1)} %broadcast_multiply_fusion, f32[8,4,64,128]{3,2,1,0:T(8,128)S(1)} %copy-done.3, f32[8,128,4]{1,0,2:T(8,128)S(1)} %convolution_add_fusion, f32[8,128,4]{1,0,2:T(8,128)S(1)} %get-tuple-element.189, s32[64]{0:T(128)S(1)} %copy-done.16, s32[8]{0:T(128)S(1)} %copy-done.13), kind=kOutput, calls=%fused_computation.36 | convolution fusion | flops 202375680 | bytes 9994528 | tf_op jit(solution)/shard_map/dg,dthe->gthe/dot_general | solution.py:185
  536.2 2.7 fusion.34
  538.9 153.4 %all-gather.3.cloned.1.call-done = f32[4096,1024]{1,0:T(8,128)} async-done(((f32[1024,1024]{1,0:T(8,128)}), f32[4096,1024]{1,0:T(8,128)}) %all-gather.3.cloned.1.call-update) | async-done | bytes 16777232 | tf_op jit(solution)/shard_map/all_gather | solution.py:196
  692.3 10.5 %reduce_sum.79 = f32[1024,1024]{1,0:T(8,128)} reduce(f32[4,1024,1024]{2,1,0:T(8,128)} %bitcast.145, f32[]{:T(128)} %constant.124.clone.1), dimensions={0}, to_apply=%region_11.12 | reduce | flops 3145728 | bytes 20971524 | tf_op jit(solution)/shard_map/reduce_sum | solution.py:196
  702.9 2.3 constant_dynamic-slice_fusion.1
  705.2 3.2 multiply_reduce_fusion
  (216 shorter events, 60.1 us)
Async XLA Ops:
  7.2 529.0 %copy-start = (bf16[256,1024]{1,0:T(8,128)(2,1)S(1)}, bf16[256,1024]{1,0:T(8,128)(2,1)}, u32[]{:S(2)}) copy-start(bf16[256,1024]{1,0:T(8,128)(2,1)} %param.30) | copy-start | bytes 1572868
  7.9 320.7 %copy-start.15 = (s32[64]{0:T(128)}, s32[64]{0:T(128)S(1)}, u32[]{:S(2)}) copy-start(s32[64]{0:T(128)S(1)} %and_select_fusion) | copy-start | bytes 772
  8.9 319.7 %copy-start.12 = (s32[8]{0:T(128)}, s32[8]{0:T(128)S(1)}, u32[]{:S(2)}) copy-start(s32[8]{0:T(128)S(1)} %slice_reduce_fusion) | copy-start | bytes 100
  9.0 23.9 %copy-start.17 = (pred[64]{0:T(512)(128)(4,1)}, pred[64]{0:T(512)(128)(4,1)S(1)}, u32[]{:S(2)}) copy-start(pred[64]{0:T(512)(128)(4,1)S(1)} %compare_and_fusion) | copy-start | bytes 196
  9.0 21.1 %copy-start.14 = (s32[1024]{0:T(1024)}, s32[1024]{0:T(1024)S(1)}, u32[]{:S(2)}) copy-start(s32[1024]{0:T(1024)S(1)} %pad_clamp_fusion) | copy-start | bytes 12292
  11.0 26.4 %all-to-all-start.1 = ((bf16[64,1,128]{2,1,0:T(2,128)(2,1)}), bf16[64,1,128]{2,1,0:T(2,128)(2,1)S(1)}, u32[]{:S(2)}, u32[]{:S(2)}) async-start(bf16[64,1,128]{2,1,0:T(2,128)(2,1)} %copy.100), calls=%async_computation.1 | async-start | bytes 65536 | tf_op jit(solution)/shard_map/all_to_all | solution.py:165
  24.9 4.8 copy-start.10
  25.0 0.5 copy-start.21
  37.4 10.7 %copy-start.26 = (s32[64]{0:T(128)S(1)}, s32[64]{0:T(128)}, u32[]{:S(2)}) copy-start(s32[64]{0:T(128)} %param.23) | copy-start | bytes 772
  37.4 13.9 %copy-start.6 = (bf16[512,256]{1,0:T(8,128)(2,1)S(1)}, bf16[512,256]{1,0:T(8,128)(2,1)}, u32[]{:S(2)}) copy-start(bf16[512,256]{1,0:T(8,128)(2,1)} %param.24) | copy-start | bytes 786436
  37.4 14.1 %copy-start.7 = (bf16[512,256]{1,0:T(8,128)(2,1)S(1)}, bf16[512,256]{1,0:T(8,128)(2,1)}, u32[]{:S(2)}) copy-start(bf16[512,256]{1,0:T(8,128)(2,1)} %param.25) | copy-start | bytes 786436
  37.4 14.3 %copy-start.27 = (s32[8]{0:T(128)S(1)}, s32[8]{0:T(128)}, u32[]{:S(2)}) copy-start(s32[8]{0:T(128)} %param.22) | copy-start | bytes 100
  37.4 14.9 %copy-start.23 = (f32[2,4]{1,0:T(2,128)S(1)}, f32[2,4]{1,0:T(2,128)}, u32[]{:S(2)}) copy-start(f32[2,4]{1,0:T(2,128)} %param.31) | copy-start | bytes 100
  37.4 106.5 %all-to-all-start = ((bf16[64,128,256]{2,1,0:T(8,128)(2,1)}), bf16[64,128,256]{2,1,0:T(8,128)(2,1)}, u32[]{:S(2)}, u32[]{:S(2)}) async-start(bf16[64,128,256]{2,1,0:T(8,128)(2,1)} %broadcast_select_fusion), calls=%async_computation | async-start | bytes 8388608 | tf_op jit(solution)/shard_map/all_to_all | solution.py:164
  156.9 12.7 %copy-start.8 = (s32[512]{0:T(512)S(1)}, s32[512]{0:T(512)}, u32[]{:S(2)}) copy-start(s32[512]{0:T(512)} %param.26) | copy-start | bytes 6148
  322.6 7.4 %copy-start.1 = (bf16[1024,1024]{1,0:T(8,128)(2,1)S(1)}, bf16[1024,1024]{1,0:T(8,128)(2,1)}, u32[]{:S(2)}) copy-start(bf16[1024,1024]{1,0:T(8,128)(2,1)} %param.18) | copy-start | bytes 6291460
  322.6 191.5 %all-to-all-start.2 = ((f32[64,128,256]{2,1,0:T(8,128)}), f32[64,128,256]{2,1,0:T(8,128)}, u32[]{:S(2)}, u32[]{:S(2)}) async-start(f32[64,128,256]{2,1,0:T(8,128)} %bitcast.147), calls=%async_computation.2 | async-start | bytes 16777216 | tf_op jit(solution)/shard_map/all_to_all | solution.py:173
  328.3 7.0 copy-start.9
  328.3 7.0 copy-start.2
  328.3 364.0 %all-gather.3.cloned.1.call-start = ((), (), s32[]{:S(2)}) async-start(), calls=%async_computation.5 | async-start | bytes 20971520 | tf_op jit(solution)/shard_map/all_gather | solution.py:196
  335.3 2.4 copy-start.24
  335.3 2.4 copy-start.25
  337.7 1.3 copy-start.4
  340.8 1.0 copy-start.5
  340.8 1.0 copy-start.18
  340.8 1.1 copy-start.13
  340.8 1.1 copy-start.16
  523.0 4.7 copy-start.3
  692.3 12.8 %copy-start.19 = (f32[1024]{0:T(1024)S(1)}, f32[1024]{0:T(1024)}, u32[]{:S(2)}) copy-start(f32[1024]{0:T(1024)} %param.33) | copy-start | bytes 12292
  692.3 12.8 %copy-start.20 = (f32[1024]{0:T(1024)S(1)}, f32[1024]{0:T(1024)}, u32[]{:S(2)}) copy-start(f32[1024]{0:T(1024)} %param.32) | copy-start | bytes 12292
  702.9 5.5 copy-start.11
  702.9 5.5 copy-start.22
Sparse Core Ops, SparseCore 0:
  539.0 153.2 all-gather.2
